TPU v7x, 32 devices: a whole 2x2x4 slice. The times are simulated.
32 devices in a mesh: dp: 8 (over z, x), tensor: 4 (over y, core).
Axes of the slice: x: 2, y: 2, z: 4, core: 2. Of those that a mesh axis runs over, the one named last changes fastest.
Arguments:
- bag_items: bfloat16 [16384, 64, 128], P('dp', 'tensor'), may hold values from -1.1953125 to 1.1953125
- bag_lengths: int32 [2048, 64], P('dp', 'tensor'), may hold values from 0 to 16, as said below
- send_counts: int32 [8, 8], P('dp'), may hold values from 0 to 48, as said below
- cross_weight: bfloat16 [1, 8192, 8192], P(None, 'tensor', 'dp'), may hold values from -0.0625 to 0.0625
- cross_bias: float32 [1, 8192], P(None, 'tensor'), may hold values from -3 to 3
Outputs:
- crossed: bfloat16 [2048, 8192], P('dp', 'tensor')
Inputs may be any that keep to these rules, and one draw needn't show every extreme that they name: `bag_lengths`: for every feature, the bags of the 256 rows of one aligned block hold 2048 items together; bags may be empty; in every aligned block and feature some bag holds exactly 16 items. `send_counts`: every row and every column sums to 256; each row has eight nonzero entries, one of them may be on the diagonal; no entry exceeds 48 and every row has an entry equal to 48.
All inputs are finite; a program needn't handle non-finite values.
Results may differ from a plain program's by a relative error of at most 0.0053.
Values may be sent and summed in bfloat16 or wider, within the bound.
No kernel may reach another device: no remote copies, remote signals or barrier semaphores. Data moves between devices by JAX's collectives and lax.ppermute only.
A program may use at most 128 MiB of HBM per device.

v0:
```python
import jax
import jax.numpy as jnp
from jax import lax
from jax.sharding import PartitionSpec as P

BAG = 8
CAP = 48


def shards(bag_items, bag_lengths, send_counts, cross_weight, cross_bias):
    row_count = bag_lengths.shape[0]
    feat_count = bag_lengths.shape[1]
    slot_count = bag_items.shape[0]
    embed_width = bag_items.shape[2]
    block_width = feat_count * embed_width
    bag_ends = jnp.cumsum(bag_lengths, axis=0)
    bag_starts = bag_ends - bag_lengths
    row_block = min(128, row_count)
    block_total = row_count // row_block
    window = min(slot_count, 2 * BAG * row_block)
    first_starts = bag_starts.reshape(block_total, row_block, feat_count)[:, 0, :]
    window_starts = jnp.clip(first_starts, 0, slot_count - window)
    feature_ids = jnp.arange(feat_count, dtype=jnp.int32)

    def take_window(start, feature):
        piece = lax.dynamic_slice(
            bag_items, (start, feature, jnp.int32(0)), (window, 1, embed_width)
        )
        return piece[:, 0, :]

    def pool_block(block_id):
        starts = window_starts[block_id]
        window_items = jax.vmap(take_window)(starts, feature_ids)
        row_first = (
            lax.dynamic_slice_in_dim(bag_starts, block_id * row_block, row_block, 0)
            - starts[None, :]
        )
        row_last = (
            lax.dynamic_slice_in_dim(bag_ends, block_id * row_block, row_block, 0) - starts[None, :]
        )
        positions = lax.broadcasted_iota(jnp.int32, (feat_count, row_block, window), 2)
        member = (positions >= row_first.T[:, :, None]) & (positions < row_last.T[:, :, None])
        one_hot = member.astype(jnp.bfloat16)
        return jnp.einsum("frs,fse->rfe", one_hot, window_items, preferred_element_type=jnp.float32)

    pooled_sum = lax.map(pool_block, jnp.arange(block_total, dtype=jnp.int32))
    pooled = pooled_sum.reshape(row_count, block_width).astype(jnp.bfloat16)
    device_count = lax.axis_size("dp")
    count_row = send_counts.reshape(-1)
    send_end = jnp.cumsum(count_row)
    send_start = send_end - count_row
    slot_ids = jnp.arange(CAP, dtype=jnp.int32)
    slot_index = jnp.minimum(send_start[:, None] + slot_ids[None, :], row_count - 1)
    slot_valid = slot_ids[None, :] < count_row[:, None]
    outgoing = jnp.where(slot_valid[:, :, None], pooled[slot_index], jnp.zeros((), jnp.bfloat16))
    received, recv_column = (
        lax.all_to_all(outgoing, "dp", split_axis=0, concat_axis=0, tiled=True),
        lax.all_to_all(
            count_row.reshape(device_count, 1), "dp", split_axis=0, concat_axis=0, tiled=True
        ),
    )
    recv_counts = recv_column.reshape(-1)
    recv_end = jnp.cumsum(recv_counts).astype(jnp.int32)
    recv_start = recv_end - recv_counts
    target_rows = jnp.arange(row_count, dtype=jnp.int32)
    source_block = jnp.sum((recv_end[None, :] <= target_rows[:, None]).astype(jnp.int32), axis=1)
    source_match = jnp.arange(device_count, dtype=jnp.int32)[None, :] == source_block[:, None]
    source_start = jnp.sum(jnp.where(source_match, recv_start[None, :], 0), axis=1)
    flat_index = source_block * CAP + target_rows - source_start
    cross_input = received.reshape(device_count * CAP, block_width)[flat_index]
    base_rows = cross_input.astype(jnp.float32)
    state = cross_input
    gathered = lax.all_gather(state, "tensor", axis=1, tiled=True)
    layer_weight = cross_weight[0]
    empty_sum = jnp.zeros((row_count, block_width), jnp.float32)
    w_piece = lax.all_gather(layer_weight, "dp", axis=1, tiled=True)
    columns = lax.slice_in_dim(gathered, 0, w_piece.shape[1], axis=1)
    product = empty_sum + lax.dot_general(
        columns, w_piece, (((1,), (1,)), ((), ())), preferred_element_type=jnp.float32
    )
    state = (base_rows * (product + cross_bias[0]) + state.astype(jnp.float32)).astype(jnp.bfloat16)
    return state


def solution(mesh):
    return jax.shard_map(
        shards,
        mesh=mesh,
        in_specs=(
            P("dp", "tensor", None),
            P("dp", "tensor"),
            P("dp", None),
            P(None, "tensor", "dp"),
            P(None, "tensor"),
        ),
        out_specs=P("dp", "tensor"),
        check_vma=False,
    )
```

profile of v0, /device:TPU:0, one launch (start us, length us, event | category | flops | bytes accessed | tf_op | source)
XLA Modules:
  0.0 814.9 jit_solution(1087858234139182849)
XLA Ops:
  6.5 1.3 copy.32
  7.9 7.3 all-to-all-start.1
  15.1 0.7 copy_bitcast_fusion.1
  15.8 0.6 reduce-window.25
  16.4 0.2 slice_reduce_fusion
  16.6 0.8 fusion.29
  17.4 0.1 bitcast_bitcast_fusion
  17.5 0.1 copy.33
  17.6 12.3 %copy.30 = bf16[2048,16,128]{0,2,1:T(8,128)(2,1)} copy(bf16[2048,16,128]{2,1,0:T(8,128)(2,1)} %param.7) | data formatting | bytes 16777216
  29.9 37.9 %while.11 = (s32[]{:T(128)}, bf16[2,128,16,128]{1,3,2,0:T(8,128)(2,1)S(1)}, s32[2]{0:T(128)S(1)}, s32[2,16]{1,0:T(2,128)S(1)}, bf16[2048,16,128]{0,2,1:T(8,128)(...) while((s32[]{:T(128)}, ...), condition=%wide.region_3.4_spmd.clone, body=%wide.region_2.3_spmd.clone.sunk | while | flops 1086328960 | bytes 26264288 | solution.py:46
  29.9 0.6 dynamic_slice.31
  32.8 0.1 subtract_bitcast_fusion.3
  32.9 8.3 %gather_fusion = bf16[16,2048,128]{1,2,0:T(8,128)(2,1)} fusion(bf16[2048,16,128]{0,2,1:T(8,128)(2,1)} %get-tuple-element.190, s32[16]{0:T(128)S(1)} %fusion.40), kind=kCustom, calls=%fused_computation.clone.clone.1 | custom fusion | bytes 16777408 | tf_op jit(solution)/shard_map/while/body/eval_jaxpr/vmap()/gather | solution.py:26
  41.1 7.8 fusion.42
  48.9 0.6 dynamic_slice.31
  51.8 0.1 subtract_bitcast_fusion.3
  51.9 8.3 %gather_fusion = bf16[16,2048,128]{1,2,0:T(8,128)(2,1)} fusion(bf16[2048,16,128]{0,2,1:T(8,128)(2,1)} %get-tuple-element.190, s32[16]{0:T(128)S(1)} %fusion.40), kind=kCustom, calls=%fused_computation.clone.clone.1 | custom fusion | bytes 16777408 | tf_op jit(solution)/shard_map/while/body/eval_jaxpr/vmap()/gather | solution.py:26
  60.1 7.8 fusion.42
  67.9 0.0 copy-start.1
  67.9 1.0 copy.31
  68.9 0.3 copy.42
  69.1 0.0 copy-done.1
  69.2 0.2 reduce-window.27
  69.3 0.1 compare_select_fusion.1
  69.4 0.1 reshape.249
  69.5 0.1 iota_compare_fusion.5
  69.6 2.4 gather_fusion.1
  72.0 1.3 broadcast_select_fusion
  73.4 0.0 all-to-all-done.1
  73.4 6.0 all-to-all-start
  79.4 0.0 all-gather.5.cloned.1.call-start
  79.4 0.2 reduce.1
  79.7 0.2 reduce-window.28
  79.8 0.1 convert_reduce_fusion
  79.9 0.1 select_reduce_fusion
  80.0 35.8 %all-to-all-done = bf16[8,48,2048]{2,1,0:T(8,128)(2,1)S(1)} async-done(((bf16[8,48,2048]{2,1,0:T(8,128)(2,1)}), bf16[8,48,2048]{2,1,0:T(8,128)(2,1)S(1)}, u32[]{:S(2)}, u32[]{:S(2)}) %all-to-all-start) | async-done | bytes 1572896 | tf_op jit(solution)/shard_map/all_to_all | solution.py:57
  115.8 2.3 gather_fusion.2
  118.1 0.0 copy-start
  118.1 0.0 copy-start.2
  118.1 0.0 all-gather.5.cloned.1.call-update
  118.2 0.0 all-gather.7.cloned.1.call-start
  118.2 0.7 all-gather.7.cloned.1.call-update
  118.9 33.0 %all-gather.5.cloned.1.call-done = bf16[256,8192]{1,0:T(8,128)(2,1)} async-done(((bf16[256,2048]{1,0:T(8,128)(2,1)}), bf16[256,8192]{1,0:T(8,128)(2,1)}) %all-gather.5.cloned.1.call-update) | async-done | bytes 4194320 | tf_op jit(solution)/shard_map/all_gather | solution.py:73
  151.9 639.3 %all-gather.7.cloned.1.call-done = bf16[1,2048,8192]{2,1,0:T(8,128)(2,1)} async-done(((bf16[1,2048,1024]{2,1,0:T(8,128)(2,1)}), bf16[1,2048,8192]{2,1,0:T(8,128)(2,1)}) %all-gather.7.cloned.1.call-update) | async-done | bytes 33554448 | tf_op jit(solution)/shard_map/all_gather | solution.py:76
  791.2 0.0 copy-done
  791.2 0.0 copy-done.2
  791.2 16.8 %fusion.26 = bf16[256,2048]{1,0:T(8,128)(2,1)} fusion(bf16[256,8192]{1,0:T(8,128)(2,1)} %all-gather.5.cloned.1.call-done, bf16[1,2048,8192]{2,1,0:T(8,128)(2,1)} %all-gather.7.cloned.1.call-done, bf16[256,2048]{1,0:T(8,128)(2,1)S(1)} %copy-done, f32[2048]{0:T(1024)S(1)} %bitcast.99), kind=kOutput, calls=%fused_computation.27 | convolution fusion | flops 8592556032 | bytes 39854080 | tf_op jit(solution)/shard_map/dot_general | solution.py:78
  (16 shorter events, 0.1 us)
Async XLA Ops:
  7.9 65.5 %all-to-all-start.1 = ((s32[8,1,1]{2,1,0:T(1,128)}), s32[8,1,1]{2,1,0:T(1,128)S(1)}, u32[]{:S(2)}, u32[]{:S(2)}) async-start(s32[8,1,1]{2,1,0:T(1,128)} %copy.32), calls=%async_computation.1 | async-start | bytes 8192 | tf_op jit(solution)/shard_map/all_to_all | solution.py:58
  67.9 1.3 copy-start.1
  73.4 42.4 %all-to-all-start = ((bf16[8,48,2048]{2,1,0:T(8,128)(2,1)}), bf16[8,48,2048]{2,1,0:T(8,128)(2,1)S(1)}, u32[]{:S(2)}, u32[]{:S(2)}) async-start(bf16[8,48,2048]{2,1,0:T(8,128)(2,1)} %broadcast_select_fusion), calls=%async_computation | async-start | bytes 3145728 | tf_op jit(solution)/shard_map/all_to_all | solution.py:57
  79.4 72.5 %all-gather.5.cloned.1.call-start = ((), (), s32[]{:S(2)}) async-start(), calls=%async_computation.2 | async-start | bytes 5242880 | tf_op jit(solution)/shard_map/all_gather | solution.py:73
  118.1 673.1 %copy-start = (bf16[256,2048]{1,0:T(8,128)(2,1)S(1)}, bf16[256,2048]{1,0:T(8,128)(2,1)}, u32[]{:S(2)}) copy-start(bf16[256,2048]{1,0:T(8,128)(2,1)} %gather_fusion.2) | copy-start | bytes 3145732
  118.1 673.1 %copy-start.2 = (f32[1,2048]{1,0:T(1,128)S(1)}, f32[1,2048]{1,0:T(1,128)}, u32[]{:S(2)}) copy-start(f32[1,2048]{1,0:T(1,128)} %param.11) | copy-start | bytes 24580
  118.2 673.0 %all-gather.7.cloned.1.call-start = ((), (), s32[]{:S(2)}) async-start(), calls=%async_computation.3 | async-start | bytes 37748736 | tf_op jit(solution)/shard_map/all_gather | solution.py:76
Sparse Core Ops, SparseCore 0:
  118.3 33.5 all-gather.4
  153.4 637.7 all-gather.6
where the time goes:
time: 816 us; the launch traced here: 815 us
  waiting for transfers between devices  709 us (87%)
  local copies, waits for them, and re-layouts  38.4 us (5%)
  matrix products  32.3 us (4%)
  between operations  13.5 us (2%)
  starting transfers between devices  13.3 us (2%)
    all_gather x1, waiting for transfers between devices, shards(): w_piece = lax.all_gather(layer_weight, 'dp', axis=1, tiled=True)  639 us
    all_to_all x1, waiting for transfers between devices, shards(): lax.all_to_all(outgoing, 'dp', split_axis=0, concat_axis=0, tiled=True)  35.8 us
    all_gather x1, waiting for transfers between devices, shards(): gathered = lax.all_gather(state, 'tensor', axis=1, tiled=True)  33 us
    dot_general x1, matrix products, shards(): lax.dot_general(columns, w_piece, (((1,), (1,)), ((), ())), preferred_ele...  16.8 us
    gather x2, local copies, waits for them, and re-layouts, take_window(): lax.dynamic_slice(bag_items, (start, feature, jnp.int32(0)), (window, 1,...  16.5 us
  transfers between devices with their start and end apart: 4, of which 3 were waited for; matrix products, arithmetic and copies ran while one was open for 7% of the time, Pallas kernels for 0%

commit v1 on v0

--- a/solution.py
+++ b/solution.py
@@ -73,7 +73,12 @@
     gathered = lax.all_gather(state, "tensor", axis=1, tiled=True)
     layer_weight = cross_weight[0]
     empty_sum = jnp.zeros((row_count, block_width), jnp.float32)
-    w_piece = lax.all_gather(layer_weight, "dp", axis=1, tiled=True)
+    ring = [layer_weight]
+    for hop in range(7):
+        ring.append(lax.ppermute(ring[-1], "dp", [(dev, (dev + 1) % 8) for dev in range(8)]))
+    w_piece = jnp.roll(
+        jnp.concatenate(ring[::-1], axis=1), (lax.axis_index("dp") + 1) * ring[0].shape[1], axis=1
+    )
     columns = lax.slice_in_dim(gathered, 0, w_piece.shape[1], axis=1)
     product = empty_sum + lax.dot_general(
         columns, w_piece, (((1,), (1,)), ((), ())), preferred_element_type=jnp.float32

time: 816 us -> 776 us (0.951); the launches traced: 815 us -> 767 us
  waiting for transfers between devices: 709 us -> 598 us
  local copies, waits for them, and re-layouts: 38.4 us -> 98.6 us
    all_gather x1 -> x0, waiting for transfers between devices: 639 us -> none  [shards(): w_piece = lax.all_gather(layer_weight, 'dp', axis=1, tiled=True)]
    ppermute x0 -> x7, waiting for transfers between devices: none -> 496 us  [shards(): lax.ppermute(ring[-1], 'dp', [(dev, (dev + 1) % 8) for dev in range(8)])]
    all_to_all x1, waiting for transfers between devices: 35.8 us -> 101 us  [shards(): lax.all_to_all(outgoing, 'dp', split_axis=0, concat_axis=0, tiled=True)]
    unnamed x9 -> x42, local copies, waits for them, and re-layouts: 12.7 us -> 70.4 us
    all_gather x1, waiting for transfers between devices: 33 us -> 0.01 us  [shards(): gathered = lax.all_gather(state, 'tensor', axis=1, tiled=True)]
  transfers between devices with their start and end apart: 4 -> 10, of which waited for: 3 -> 7; matrix products, arithmetic and copies ran while one was open for 7% -> 14% of each run, Pallas kernels for 0% -> 0%
where the time goes in v1:
time: 776 us; the launch traced here: 767 us
  waiting for transfers between devices  598 us (77%)
  local copies, waits for them, and re-layouts  98.6 us (13%)
  matrix products  32.6 us (4%)
  starting transfers between devices  15.2 us (2%)
  between operations  13.5 us (2%)
    ppermute x7, waiting for transfers between devices, shards(): lax.ppermute(ring[-1], 'dp', [(dev, (dev + 1) % 8) for dev in range(8)])  496 us
    all_to_all x1, waiting for transfers between devices, shards(): lax.all_to_all(outgoing, 'dp', split_axis=0, concat_axis=0, tiled=True)  101 us
    unnamed x42, local copies, waits for them, and re-layouts  70.4 us
    dot_general x1, matrix products, shards(): lax.dot_general(columns, w_piece, (((1,), (1,)), ((), ())), preferred_ele...  17.1 us
    gather x2, local copies, waits for them, and re-layouts, take_window(): lax.dynamic_slice(bag_items, (start, feature, jnp.int32(0)), (window, 1,...  16.5 us
  transfers between devices with their start and end apart: 10, of which 7 were waited for; matrix products, arithmetic and copies ran while one was open for 14% of the time, Pallas kernels for 0%

profile of v1, /device:TPU:0, one launch (start us, length us, event | category | flops | bytes accessed | tf_op | source)
XLA Modules:
  0.0 766.5 jit_solution(3271563085243722938)
XLA Ops:
  6.5 2.9 collective-permute-start
  9.5 93.8 %collective-permute-done = bf16[2048,1024]{1,0:T(8,128)(2,1)S(1)} collective-permute-done((bf16[2048,1024]{1,0:T(8,128)(2,1)}, bf16[2048,1024]{1,0:T(8,128)(2,1)S(1)}, u32[]{:S(2)}, u32[]{:S(2)}) %collective-permute-start) | collective-permute-done | bytes 4194336 | tf_op jit(solution)/shard_map/ppermute | solution.py:78
  103.3 2.0 copy-done.1
  105.3 94.5 %collective-permute-done.1 = bf16[2048,1024]{1,0:T(8,128)(2,1)S(1)} collective-permute-done((bf16[2048,1024]{1,0:T(8,128)(2,1)S(1)}, bf16[2048,1024]{1,0:T(8,128)(2,1)S(1)}, u32[]{:S(2)}, u32[]{:S(2)}) %collective-permute-start.1) | collective-permute-done | bytes 4194336 | tf_op jit(solution)/shard_map/ppermute | solution.py:78
  199.7 2.0 copy-done.3
  201.7 93.5 %collective-permute-done.2 = bf16[2048,1024]{1,0:T(8,128)(2,1)S(1)} collective-permute-done((bf16[2048,1024]{1,0:T(8,128)(2,1)S(1)}, bf16[2048,1024]{1,0:T(8,128)(2,1)S(1)}, u32[]{:S(2)}, u32[]{:S(2)}) %collective-permute-start.2) | collective-permute-done | bytes 4194336 | tf_op jit(solution)/shard_map/ppermute | solution.py:78
  295.3 1.9 copy-done.5
  297.2 92.6 %collective-permute-done.3 = bf16[2048,1024]{1,0:T(8,128)(2,1)S(1)} collective-permute-done((bf16[2048,1024]{1,0:T(8,128)(2,1)S(1)}, bf16[2048,1024]{1,0:T(8,128)(2,1)S(1)}, u32[]{:S(2)}, u32[]{:S(2)}) %collective-permute-start.3) | collective-permute-done | bytes 4194336 | tf_op jit(solution)/shard_map/ppermute | solution.py:78
  389.8 2.0 copy-done.7
  391.8 91.8 %collective-permute-done.4 = bf16[2048,1024]{1,0:T(8,128)(2,1)} collective-permute-done((bf16[2048,1024]{1,0:T(8,128)(2,1)S(1)}, bf16[2048,1024]{1,0:T(8,128)(2,1)}, u32[]{:S(2)}, u32[]{:S(2)}) %collective-permute-start.4) | collective-permute-done | bytes 4194336 | tf_op jit(solution)/shard_map/ppermute | solution.py:78
  483.6 1.3 copy.32
  484.9 6.0 all-to-all-start.1
  490.9 0.7 copy_bitcast_fusion.1
  491.6 0.6 reduce-window.25
  492.4 0.8 fusion.30
  493.3 12.4 %copy.30 = bf16[2048,16,128]{0,2,1:T(8,128)(2,1)} copy(bf16[2048,16,128]{2,1,0:T(8,128)(2,1)} %param.7) | data formatting | bytes 16777216
  506.0 38.5 %while.11 = (s32[]{:T(128)}, bf16[2,128,16,128]{1,3,2,0:T(8,128)(2,1)S(1)}, s32[2]{0:T(128)S(1)}, s32[2,16]{1,0:T(2,128)S(1)}, bf16[2048,16,128]{0,2,1:T(8,128)(...) while((s32[]{:T(128)}, ...), condition=%wide.region_3.4_spmd.clone, body=%wide.region_2.3_spmd.clone.sunk | while | flops 1086328960 | bytes 26264288 | solution.py:46
  506.0 0.6 dynamic_slice.44
  509.2 8.3 %gather_fusion = bf16[16,2048,128]{1,2,0:T(8,128)(2,1)} fusion(bf16[2048,16,128]{0,2,1:T(8,128)(2,1)} %get-tuple-element.190, s32[16]{0:T(128)S(1)} %fusion.41), kind=kCustom, calls=%fused_computation.clone.clone.1 | custom fusion | bytes 16777408 | tf_op jit(solution)/shard_map/while/body/eval_jaxpr/vmap()/gather | solution.py:26
  517.5 7.8 %fusion.43 = bf16[2,128,16,128]{1,3,2,0:T(8,128)(2,1)S(1)} fusion(bf16[2,128,16,128]{1,3,2,0:T(8,128)(2,1)S(1)} %get-tuple-element.175, s32[]{:T(128)} %get-tuple-element.174, bf16[16,2048,128]{1,2,0:T(8,128)(2,1)} %gather_fusion, s32[16,128]{1,0:T(8,128)S(1)} %get-tuple-element.160, s32[16,128]{1,0:T(8,128)S(1)} %get-tuple-element.161), kind=kOutput, calls=%fused_computation.11.clone.1 | convolution fusion | flops 1086324736 | bytes 9453572 | tf_op jit(solution)/shard_map/while/body/eval_jaxpr/frs,fse->rfe/dot_general | solution.py:44
  525.3 0.6 dynamic_slice.44
  528.5 8.3 %gather_fusion = bf16[16,2048,128]{1,2,0:T(8,128)(2,1)} fusion(bf16[2048,16,128]{0,2,1:T(8,128)(2,1)} %get-tuple-element.190, s32[16]{0:T(128)S(1)} %fusion.41), kind=kCustom, calls=%fused_computation.clone.clone.1 | custom fusion | bytes 16777408 | tf_op jit(solution)/shard_map/while/body/eval_jaxpr/vmap()/gather | solution.py:26
  536.7 7.8 %fusion.43 = bf16[2,128,16,128]{1,3,2,0:T(8,128)(2,1)S(1)} fusion(bf16[2,128,16,128]{1,3,2,0:T(8,128)(2,1)S(1)} %get-tuple-element.175, s32[]{:T(128)} %get-tuple-element.174, bf16[16,2048,128]{1,2,0:T(8,128)(2,1)} %gather_fusion, s32[16,128]{1,0:T(8,128)S(1)} %get-tuple-element.160, s32[16,128]{1,0:T(8,128)S(1)} %get-tuple-element.161), kind=kOutput, calls=%fused_computation.11.clone.1 | convolution fusion | flops 1086324736 | bytes 9453572 | tf_op jit(solution)/shard_map/while/body/eval_jaxpr/frs,fse->rfe/dot_general | solution.py:44
  544.5 30.2 %collective-permute-done.5 = bf16[2048,1024]{1,0:T(8,128)(2,1)} collective-permute-done((bf16[2048,1024]{1,0:T(8,128)(2,1)}, bf16[2048,1024]{1,0:T(8,128)(2,1)}, u32[]{:S(2)}, u32[]{:S(2)}) %collective-permute-start.5) | collective-permute-done | bytes 4194336 | tf_op jit(solution)/shard_map/ppermute | solution.py:78
  574.7 1.0 copy.31
  575.7 0.3 copy.42
  576.2 2.5 gather_fusion.1
  578.7 1.4 broadcast_select_fusion
  580.1 6.0 all-to-all-start
  587.0 101.1 %all-to-all-done = bf16[8,48,2048]{2,1,0:T(8,128)(2,1)S(1)} async-done(((bf16[8,48,2048]{2,1,0:T(8,128)(2,1)}), bf16[8,48,2048]{2,1,0:T(8,128)(2,1)S(1)}, u32[]{:S(2)}, u32[]{:S(2)}) %all-to-all-start) | async-done | bytes 1572896 | tf_op jit(solution)/shard_map/all_to_all | solution.py:57
  688.0 2.3 gather_fusion.2
  690.4 4.5 constant_dynamic-update-slice_fusion.15
  694.9 4.7 constant_dynamic-update-slice_fusion.14
  699.7 4.7 constant_dynamic-update-slice_fusion.13
  704.4 2.7 constant_dynamic-update-slice_fusion.12
  707.0 2.6 constant_dynamic-update-slice_fusion.11
  709.6 2.6 constant_dynamic-update-slice_fusion.10
  712.2 2.4 constant_dynamic-update-slice_fusion.9
  714.6 2.4 constant_dynamic-update-slice_fusion.8
  717.0 4.5 constant_dynamic-update-slice_fusion.7
  721.5 4.6 constant_dynamic-update-slice_fusion.6
  726.1 4.6 constant_dynamic-update-slice_fusion.5
  730.7 2.4 constant_dynamic-update-slice_fusion.4
  733.1 2.4 constant_dynamic-update-slice_fusion.3
  735.4 2.4 constant_dynamic-update-slice_fusion.2
  737.8 2.4 constant_dynamic-update-slice_fusion.1
  740.2 2.4 constant_dynamic-update-slice_fusion
  742.5 17.1 %fusion.26 = bf16[256,2048]{1,0:T(8,128)(2,1)} fusion(bf16[256,8192]{1,0:T(8,128)(2,1)} %all-gather.3.cloned.1.call-done, bf16[2048,16384]{1,0:T(8,128)(2,1)} %constant_dynamic-update-slice_fusion, s32[]{:T(128)S(6)} %select_n.73, bf16[256,2048]{1,0:T(8,128)(2,1)S(1)} %copy-done.9, f32[2048]{0:T(1024)S(1)} %bitcast.94), kind=kOutput, calls=%fused_computation.27 | convolution fusion | flops 8592556032 | bytes 39854084 | tf_op jit(solution)/shard_map/dot_general | solution.py:83
  (60 shorter events, 1.9 us)
Async XLA Ops:
  6.5 96.8 %collective-permute-start = (bf16[2048,1024]{1,0:T(8,128)(2,1)}, bf16[2048,1024]{1,0:T(8,128)(2,1)S(1)}, u32[]{:S(2)}, u32[]{:S(2)}) collective-permute-start(bf16[2048,1024]{1,0:T(8,128)(2,1)} %bitcast.83), channel_id=1, source_target_pairs={{0,4},{4,8},{8,12},{12,16},{16,20},{20,24},{24,28},{28,0},{1,5},{5... | collective-permute-start | bytes 12582920 | tf_op jit(solution)/shard_map/ppermute | solution.py:78
  103.3 2.0 copy-start.1
  105.3 94.5 %collective-permute-start.1 = (bf16[2048,1024]{1,0:T(8,128)(2,1)S(1)}, bf16[2048,1024]{1,0:T(8,128)(2,1)S(1)}, u32[]{:S(2)}, u32[]{:S(2)}) collective-permute-start(bf16[2048,1024]{1,0:T(8,128)(2,1)S(1)} %collective-permute-done), channel_id=1, source_target_pairs={{0,4},{4,8},{8,12},{12,16},{16,20},{20,24},{24,28},{28,0},{1,5},{5... | collective-permute-start | bytes 12582920 | tf_op jit(solution)/shard_map/ppermute | solution.py:78
  199.7 2.0 copy-start.3
  201.7 93.5 %collective-permute-start.2 = (bf16[2048,1024]{1,0:T(8,128)(2,1)S(1)}, bf16[2048,1024]{1,0:T(8,128)(2,1)S(1)}, u32[]{:S(2)}, u32[]{:S(2)}) collective-permute-start(bf16[2048,1024]{1,0:T(8,128)(2,1)S(1)} %collective-permute-done.1), channel_id=1, source_target_pairs={{0,4},{4,8},{8,12},{12,16},{16,20},{20,24},{24,28},{28,0},{1,5},{5... | collective-permute-start | bytes 12582920 | tf_op jit(solution)/shard_map/ppermute | solution.py:78
  295.2 2.0 copy-start.5
  297.2 92.6 %collective-permute-start.3 = (bf16[2048,1024]{1,0:T(8,128)(2,1)S(1)}, bf16[2048,1024]{1,0:T(8,128)(2,1)S(1)}, u32[]{:S(2)}, u32[]{:S(2)}) collective-permute-start(bf16[2048,1024]{1,0:T(8,128)(2,1)S(1)} %collective-permute-done.2), channel_id=1, source_target_pairs={{0,4},{4,8},{8,12},{12,16},{16,20},{20,24},{24,28},{28,0},{1,5},{5... | collective-permute-start | bytes 12582920 | tf_op jit(solution)/shard_map/ppermute | solution.py:78
  389.8 2.0 copy-start.7
  391.8 91.8 %collective-permute-start.4 = (bf16[2048,1024]{1,0:T(8,128)(2,1)S(1)}, bf16[2048,1024]{1,0:T(8,128)(2,1)}, u32[]{:S(2)}, u32[]{:S(2)}) collective-permute-start(bf16[2048,1024]{1,0:T(8,128)(2,1)S(1)} %collective-permute-done.3), channel_id=1, source_target_pairs={{0,4},{4,8},{8,12},{12,16},{16,20},{20,24},{24,28},{28,0},{1,5},{5... | collective-permute-start | bytes 12582920 | tf_op jit(solution)/shard_map/ppermute | solution.py:78
  483.6 91.1 %collective-permute-start.5 = (bf16[2048,1024]{1,0:T(8,128)(2,1)}, bf16[2048,1024]{1,0:T(8,128)(2,1)}, u32[]{:S(2)}, u32[]{:S(2)}) collective-permute-start(bf16[2048,1024]{1,0:T(8,128)(2,1)} %collective-permute-done.4), channel_id=1, source_target_pairs={{0,4},{4,8},{8,12},{12,16},{16,20},{20,24},{24,28},{28,0},{1,5},{5... | collective-permute-start | bytes 12582920 | tf_op jit(solution)/shard_map/ppermute | solution.py:78
  484.9 95.2 %all-to-all-start.1 = ((s32[8,1,1]{2,1,0:T(1,128)}), s32[8,1,1]{2,1,0:T(1,128)S(1)}, u32[]{:S(2)}, u32[]{:S(2)}) async-start(s32[8,1,1]{2,1,0:T(1,128)} %copy.32), calls=%async_computation.1 | async-start | bytes 8192 | tf_op jit(solution)/shard_map/all_to_all | solution.py:58
  493.3 12.4 %copy-start.10 = (s32[1,8]{1,0:T(1,128)S(1)}, s32[1,8]{1,0:T(1,128)}, u32[]{:S(2)}) copy-start(s32[1,8]{1,0:T(1,128)} %param.9) | copy-start | bytes 100
  574.7 115.7 %collective-permute-start.6 = (bf16[2048,1024]{1,0:T(8,128)(2,1)}, bf16[2048,1024]{1,0:T(8,128)(2,1)}, u32[]{:S(2)}, u32[]{:S(2)}) collective-permute-start(bf16[2048,1024]{1,0:T(8,128)(2,1)} %collective-permute-done.5), channel_id=1, source_target_pairs={{0,4},{4,8},{8,12},{12,16},{16,20},{20,24},{24,28},{28,0},{1,5},{5... | collective-permute-start | bytes 12582920 | tf_op jit(solution)/shard_map/ppermute | solution.py:78
  580.1 107.9 %all-to-all-start = ((bf16[8,48,2048]{2,1,0:T(8,128)(2,1)}), bf16[8,48,2048]{2,1,0:T(8,128)(2,1)S(1)}, u32[]{:S(2)}, u32[]{:S(2)}) async-start(bf16[8,48,2048]{2,1,0:T(8,128)(2,1)} %broadcast_select_fusion), calls=%async_computation | async-start | bytes 3145728 | tf_op jit(solution)/shard_map/all_to_all | solution.py:57
  586.1 156.4 %all-gather.3.cloned.1.call-start = ((), (), s32[]{:S(2)}) async-start(), calls=%async_computation.2 | async-start | bytes 5242880 | tf_op jit(solution)/shard_map/all_gather | solution.py:73
  694.9 9.5 %copy-start.8 = (bf16[2048,1024]{1,0:T(8,128)(2,1)S(1)}, bf16[2048,1024]{1,0:T(8,128)(2,1)}, u32[]{:S(2)}) copy-start(bf16[2048,1024]{1,0:T(8,128)(2,1)} %copy-done.7) | copy-start | bytes 12582916
  699.7 7.4 copy-start.6
  704.4 5.3 copy-start.4
  707.0 5.2 copy-start.2
  709.6 5.0 copy-start
  737.8 4.7 copy-start.9
  737.8 4.7 copy-start.11
Sparse Core Ops, SparseCore 0:
  690.5 41.2 all-gather.2
